TPU v7x, 256 devices: a whole 4x4x8 slice. The times are simulated.
256 devices in a mesh: row: 16 (over z_hi, y, core), col: 16 (over z_lo, x).
Axes of the slice: x: 4, y: 4, z: 8 (z_hi: 2, z_lo: 4; z = z_hi * 4 + z_lo), core: 2. Of those that a mesh axis runs over, the one named last changes fastest.
Arguments:
- tokens: bfloat16 [2048, 8192], P('col', 'row'), may hold values from -6 to 6
- gate_vals: bfloat16 [448, 64, 4096], P('col', 'row'), may hold values from -0.09375 to 0.09375
- gate_scales: float32 [448, 64], P('col', 'row'), may hold values from 0.3 to 3
- gate_rows: int32 [448, 64], P('col', 'row'), may hold values from 0 to 127, as said below
- up_vals: bfloat16 [448, 64, 4096], P('col', 'row'), may hold values from -0.09375 to 0.09375
- up_scales: float32 [448, 64], P('col', 'row'), may hold values from 0.3 to 3
- up_rows: int32 [448, 64], P('col', 'row'), may hold values from 0 to 127, as said below
- down_vals: bfloat16 [128, 224, 4096], P('row', 'col'), may hold values from -0.046875 to 0.046875
- down_scales: float32 [128, 224], P('row', 'col'), may hold values from 0.3 to 3
- down_rows: int32 [128, 224], P('row', 'col'), may hold values from 0 to 447, as said below
Outputs:
- mixed: bfloat16 [2048, 8192], P('col', 'row')
Inputs may be any that keep to these rules, and one draw needn't show every extreme that they name: Row j of gate_rows holds distinct block rows; slots k with the same k // 4 hold exactly half of the block rows from (k // 4) * 8 to that plus 8 - 1, in increasing order. `up_rows`: same law as gate_rows, drawn independently. Row j of down_rows holds distinct block rows of the hidden units; slots k with the same k // 14 hold exactly half of the block rows from (k // 14) * 28 to that plus 28 - 1, in increasing order.
All inputs are finite; a program needn't handle non-finite values.
Results may differ from a plain program's by a relative error of at most 0.03.
Values may be sent and summed in bfloat16 or wider, within the bound.
A program may use at most 128 MiB of HBM per device.

v0:
```python
import jax
import jax.numpy as jnp
from jax import lax
from jax.sharding import PartitionSpec as P

BLOCK = 64


def dense_panel(values, scales, indices, offset, groups):
    blocks = (values.astype(jnp.float32) * scales[:, :, None]).astype(jnp.bfloat16)
    onehot = (
        indices[:, :, None] - offset == jnp.arange(groups, dtype=jnp.int32)[None, None, :]
    ).astype(jnp.bfloat16)
    matrix = jnp.einsum("jkg,jkc->gjc", onehot, blocks, preferred_element_type=jnp.float32).astype(
        jnp.bfloat16
    )
    matrix = matrix.reshape(groups, values.shape[0], BLOCK, BLOCK).transpose(0, 2, 1, 3)
    return matrix.reshape(groups * BLOCK, values.shape[0] * BLOCK)


def swish_gate(summed, ff_local):
    return (jax.nn.silu(summed[:, :ff_local]) * summed[:, ff_local:]).astype(jnp.bfloat16)


def per_device(
    tokens,
    gate_vals,
    gate_scales,
    gate_rows,
    up_vals,
    up_scales,
    up_rows,
    down_vals,
    down_scales,
    down_rows,
):
    group_size = tokens.shape[1] // BLOCK
    row_offset = lax.axis_index("row") * group_size
    w_gate = dense_panel(gate_vals, gate_scales, gate_rows, row_offset, group_size)
    w_up = dense_panel(up_vals, up_scales, up_rows, row_offset, group_size)
    joined = jnp.concatenate([w_gate, w_up], axis=1)
    ff_local = w_gate.shape[1]
    ff_groups = ff_local // BLOCK
    w_down = dense_panel(
        down_vals, down_scales, down_rows, lax.axis_index("col") * ff_groups, ff_groups
    )
    gathered = lax.all_gather(tokens, "col", axis=0, tiled=True)
    selected = gathered
    summed = lax.psum_scatter(
        jnp.dot(selected, joined, preferred_element_type=jnp.float32).astype(jnp.bfloat16),
        "row",
        scatter_dimension=0,
        tiled=True,
    ).astype(jnp.float32)
    hidden_part = swish_gate(summed, ff_local)
    hidden = lax.all_gather(hidden_part, "row", axis=0, tiled=True)
    selected = hidden
    return lax.psum_scatter(
        jnp.dot(selected, w_down, preferred_element_type=jnp.float32).astype(jnp.bfloat16),
        "col",
        scatter_dimension=0,
        tiled=True,
    )


def solution(mesh):
    placed = (
        P("col", "row"),
        P("col", "row", None),
        P("col", "row"),
        P("col", "row"),
        P("col", "row", None),
        P("col", "row"),
        P("col", "row"),
        P("row", "col", None),
        P("row", "col"),
        P("row", "col"),
    )
    return jax.shard_map(
        per_device, mesh=mesh, in_specs=placed, out_specs=P("col", "row"), check_vma=False
    )
```

profile of v0, /device:TPU:8, one launch (start us, length us, event | category | flops | bytes accessed | tf_op | source)
XLA Modules:
  0.0 520.2 jit_solution(7833358821904089959)
XLA Ops:
  6.5 0.7 all-gather.3.cloned.1.call-update
  8.1 0.8 copy.27
  8.9 2.4 fusion.2
  11.3 4.9 reshape.27
  16.2 6.2 %copy.29 = bf16[8,28,64,64]{2,0,3,1:T(8,128)(2,1)} copy(bf16[8,28,64,64]{3,2,0,1:T(8,128)(2,1)} %reshape.27) | data formatting | bytes 3670016 | tf_op jit(solution)/shard_map/reshape | solution.py:17
  22.4 5.1 reshape.28
  27.7 2.5 fusion.3
  30.2 6.3 %reshape.29 = bf16[8,28,64,64]{3,2,0,1:T(8,128)(2,1)} reshape(bf16[8,28,4096]{2,0,1:T(8,128)(2,1)} %fusion.3) | data formatting | bytes 3670016 | tf_op jit(solution)/shard_map/reshape | solution.py:17
  36.6 6.2 %copy.32 = bf16[8,28,64,64]{2,0,3,1:T(8,128)(2,1)} copy(bf16[8,28,64,64]{3,2,0,1:T(8,128)(2,1)} %reshape.29) | data formatting | bytes 3670016 | tf_op jit(solution)/shard_map/reshape | solution.py:17
  42.8 5.9 %reshape.30 = bf16[512,1792]{0,1:T(8,128)(2,1)} reshape(bf16[8,64,28,64]{1,0,3,2:T(8,128)(2,1)} %bitcast.30) | data formatting | bytes 3670016 | tf_op jit(solution)/shard_map/reshape | solution.py:18
  48.7 46.1 %all-gather.3.cloned.1.call-done = bf16[2048,512]{1,0:T(8,128)(2,1)} async-done(((bf16[128,512]{1,0:T(8,128)(2,1)}), bf16[2048,512]{1,0:T(8,128)(2,1)}) %all-gather.3.cloned.1.call-update) | async-done | bytes 2097168 | tf_op jit(solution)/shard_map/all_gather | solution.py:47
  94.8 12.9 %fusion = bf16[2048,3584]{0,1:T(8,128)(2,1)} fusion(bf16[2048,512]{1,0:T(8,128)(2,1)} %all-gather.3.cloned.1.call-done, bf16[512,1792]{0,1:T(8,128)(2,1)} %reshape.30, bf16[512,1792]{0,1:T(8,128)(2,1)S(1)} %reshape.28), kind=kOutput, calls=%fused_computation.1 | convolution fusion | flops 7530872832 | bytes 20447232 | tf_op jit(solution)/shard_map/dot_general | solution.py:50
  107.6 18.7 %copy.37 = bf16[2048,3584]{1,0:T(8,128)(2,1)} copy(bf16[2048,3584]{0,1:T(8,128)(2,1)} %fusion) | data formatting | bytes 29360128
  126.4 191.3 %reduce-scatter.7.cloned.1.call-done = bf16[128,3584]{1,0:T(8,128)(2,1)} async-done(((bf16[2048,3584]{1,0:T(8,128)(2,1)}), bf16[128,3584]{1,0:T(8,128)(2,1)}) %reduce-scatter.7.cloned.1.call-update) | async-done | bytes 917520
  317.8 1.5 copy.38
  319.5 1.0 fusion.8
  321.1 1.3 fusion.1
  322.5 1.0 copy.35
  323.5 5.0 reshape.31
  328.4 7.5 %copy.36 = bf16[28,64,8,64]{3,2,1,0:T(8,128)(2,1)} copy(bf16[28,64,8,64]{3,1,2,0:T(8,128)(2,1)} %bitcast.31) | data formatting | bytes 3670016 | tf_op jit(solution)/shard_map/transpose | solution.py:17
  336.0 5.0 reshape.32
  341.0 79.6 %all-gather.5.cloned.1.call-done = bf16[2048,1792]{0,1:T(8,128)(2,1)} async-done(((bf16[128,1792]{0,1:T(8,128)(2,1)}), bf16[2048,1792]{0,1:T(8,128)(2,1)}) %all-gather.5.cloned.1.call-update) | async-done | bytes 7340048 | tf_op jit(solution)/shard_map/all_gather | solution.py:56
  420.6 8.5 %convolution_convert_fusion.4 = bf16[2048,512]{1,0:T(8,128)(2,1)} fusion(bf16[2048,1792]{0,1:T(8,128)(2,1)} %all-gather.5.cloned.1.call-done, bf16[1792,512]{1,0:T(8,128)(2,1)S(1)} %reshape.32), kind=kOutput, calls=%fused_computation.11 | convolution fusion | flops 3759144960 | bytes 11272192 | tf_op jit(solution)/shard_map/dot_general | solution.py:59
  429.1 84.5 %reduce-scatter.5.cloned.1.call-done = bf16[128,512]{1,0:T(8,128)(2,1)} async-done(((bf16[2048,512]{1,0:T(8,128)(2,1)}), bf16[128,512]{1,0:T(8,128)(2,1)}) %reduce-scatter.5.cloned.1.call-update) | async-done | bytes 131088 | tf_op jit(solution)/shard_map/reduce_scatter | solution.py:58
  (25 shorter events, 1.8 us)
Async XLA Ops:
  6.5 88.2 %all-gather.3.cloned.1.call-start = ((), (), s32[]{:S(2)}) async-start(), calls=%async_computation.2 | async-start | bytes 2228224 | tf_op jit(solution)/shard_map/all_gather | solution.py:47
  7.3 310.5 %reduce-scatter.7.cloned.1.call-start = ((), (), s32[]{:S(2)}) async-start(), calls=%async_computation.5 | async-start | bytes 15597568
  22.4 5.2 %copy-start.3 = (f32[28,4]{0,1:T(4,128)S(1)}, f32[28,4]{0,1:T(4,128)}, u32[]{:S(2)}) copy-start(f32[28,4]{0,1:T(4,128)} %param.15) | copy-start | bytes 1348
  22.4 5.3 %copy-start.4 = (bf16[28,4,4096]{2,1,0:T(4,128)(2,1)S(1)}, bf16[28,4,4096]{2,1,0:T(4,128)(2,1)}, u32[]{:S(2)}) copy-start(bf16[28,4,4096]{2,1,0:T(4,128)(2,1)} %param.14) | copy-start | bytes 2752516
  126.4 294.2 %all-gather.5.cloned.1.call-start = ((), (), s32[]{:S(2)}) async-start(), calls=%async_computation.3 | async-start | bytes 7798784 | tf_op jit(solution)/shard_map/all_gather | solution.py:56
  319.3 1.5 copy-start.1
  319.4 1.5 copy-start.2
  319.4 1.5 copy-start
  320.6 193.1 %reduce-scatter.5.cloned.1.call-start = ((), (), s32[]{:S(2)}) async-start(), calls=%async_computation.4 | async-start | bytes 2228224 | tf_op jit(solution)/shard_map/reduce_scatter | solution.py:58
Sparse Core Ops, SparseCore 0:
  9.1 85.6 all-gather.2
  126.5 191.2 reduce-scatter.6
  320.7 99.8 all-gather.4
  429.3 84.3 reduce-scatter.4
where the time goes:
time: 522 us; the launch traced here: 520 us
  waiting for transfers between devices  402 us (77%)
  local copies, waits for them, and re-layouts  74.7 us (14%)
  matrix products  27.6 us (5%)
  between operations  13.2 us (3%)
    unnamed x5, waiting for transfers between devices  192 us
    reduce_scatter x1, waiting for transfers between devices, per_device(): lax.psum_scatter(jnp.dot(selected, w_down, preferred_element_type=jnp.flo...  84.5 us
    all_gather x1, waiting for transfers between devices, per_device(): hidden = lax.all_gather(hidden_part, 'row', axis=0, tiled=True)  79.6 us
    all_gather x1, waiting for transfers between devices, per_device(): gathered = lax.all_gather(tokens, 'col', axis=0, tiled=True)  46.1 us
    reshape x5, local copies, waits for them, and re-layouts, dense_panel(): matrix.reshape(groups, values.shape[0], BLOCK, BLOCK).transpose(0, 2, 1, 3)  28.6 us
    unnamed x15, local copies, waits for them, and re-layouts  21.3 us
    reshape x3, local copies, waits for them, and re-layouts, dense_panel(): return matrix.reshape(groups * BLOCK, values.shape[0] * BLOCK)  16 us
    dot_general x1, matrix products, per_device(): jnp.dot(selected, joined, preferred_element_type=jnp.float32)  12.9 us
  transfers between devices with their start and end apart: 4, of which 4 were waited for; matrix products, arithmetic and copies ran while one was open for 12% of the time, Pallas kernels for 0%

commit v1 on v0

--- a/solution.py
+++ b/solution.py
@@ -4,6 +4,15 @@
 from jax.sharding import PartitionSpec as P
 
 BLOCK = 64
+follow_ports = lambda my_data: jnp.concatenate(
+    lax.all_to_all(
+        jnp.stack([my_data for _ in range(lax.axis_size("col"))]),
+        "col",
+        split_axis=0,
+        concat_axis=0,
+    ),
+    axis=0,
+)
 
 
 def dense_panel(values, scales, indices, offset, groups):
@@ -44,7 +53,7 @@
     w_down = dense_panel(
         down_vals, down_scales, down_rows, lax.axis_index("col") * ff_groups, ff_groups
     )
-    gathered = lax.all_gather(tokens, "col", axis=0, tiled=True)
+    gathered = follow_ports(tokens)
     selected = gathered
     summed = lax.psum_scatter(
         jnp.dot(selected, joined, preferred_element_type=jnp.float32).astype(jnp.bfloat16),

time: 522 us -> 495 us (0.948)
  waiting for transfers between devices: 402 us -> 363 us
  starting transfers between devices: 0.31 us -> 8.91 us
    all_gather x1 -> x0, waiting for transfers between devices: 46.1 us -> none  [per_device(): gathered = lax.all_gather(tokens, 'col', axis=0, tiled=True)]
    all_to_all x0 -> x1, starting transfers between devices: none -> 8.61 us  [lax.all_to_all(jnp.stack([my_data for _ in range(lax.axis_size('col'))]),...]
    unnamed x5 -> x4, waiting for transfers between devices: 192 us -> 198 us
    unnamed x15 -> x23, local copies, waits for them, and re-layouts: 21.3 us -> 20.7 us
  transfers between devices with their start and end apart: 4 -> 4, of which waited for: 4 -> 4; matrix products, arithmetic and copies ran while one was open for 12% -> 13% of each run, Pallas kernels for 0% -> 0%
where the time goes in v1:
time: 495 us; the launch traced here: 493 us
  waiting for transfers between devices  363 us (73%)
  local copies, waits for them, and re-layouts  78.8 us (16%)
  matrix products  27.9 us (6%)
  between operations  13.2 us (3%)
  starting transfers between devices  8.91 us (2%)
    unnamed x4, waiting for transfers between devices  198 us
    reduce_scatter x1, waiting for transfers between devices, per_device(): lax.psum_scatter(jnp.dot(selected, w_down, preferred_element_type=jnp.flo...  84.5 us
    all_gather x1, waiting for transfers between devices, per_device(): hidden = lax.all_gather(hidden_part, 'row', axis=0, tiled=True)  79.6 us
    reshape x5, local copies, waits for them, and re-layouts, dense_panel(): matrix.reshape(groups, values.shape[0], BLOCK, BLOCK).transpose(0, 2, 1, 3)  29.9 us
    unnamed x23, local copies, waits for them, and re-layouts  20.7 us
    reshape x3, local copies, waits for them, and re-layouts, dense_panel(): return matrix.reshape(groups * BLOCK, values.shape[0] * BLOCK)  16.9 us
    dot_general x1, matrix products, per_device(): jnp.dot(selected, joined, preferred_element_type=jnp.float32)  13.1 us
  transfers between devices with their start and end apart: 4, of which 4 were waited for; matrix products, arithmetic and copies ran while one was open for 13% of the time, Pallas kernels for 0%

profile of v1, /device:TPU:8, one launch (start us, length us, event | category | flops | bytes accessed | tf_op | source)
XLA Modules:
  0.0 493.1 jit_solution(4012081200027790918)
XLA Ops:
  6.5 2.5 stack.2
  9.1 8.6 %all-to-all-start = ((bf16[16,128,512]{2,1,0:T(8,128)(2,1)}), bf16[16,128,512]{2,1,0:T(8,128)(2,1)S(1)}, u32[]{:S(2)}, u32[]{:S(2)}) async-start(bf16[16,128,512]{2,1,0:T(8,128)(2,1)} %stack.2), calls=%async_computation | async-start | bytes 4194304 | tf_op jit(solution)/shard_map/all_to_all | solution.py:8
  18.0 2.5 fusion.2
  20.4 6.3 %reshape.32 = bf16[8,28,64,64]{3,2,0,1:T(8,128)(2,1)} reshape(bf16[8,28,4096]{2,0,1:T(8,128)(2,1)} %fusion.2) | data formatting | bytes 3670016 | tf_op jit(solution)/shard_map/reshape | solution.py:26
  26.8 6.2 %copy.29 = bf16[8,28,64,64]{2,0,3,1:T(8,128)(2,1)} copy(bf16[8,28,64,64]{3,2,0,1:T(8,128)(2,1)} %reshape.32) | data formatting | bytes 3670016 | tf_op jit(solution)/shard_map/reshape | solution.py:26
  33.0 6.0 %reshape.33 = bf16[512,1792]{0,1:T(8,128)(2,1)} reshape(bf16[8,64,28,64]{1,0,3,2:T(8,128)(2,1)} %bitcast.30) | data formatting | bytes 3670016 | tf_op jit(solution)/shard_map/reshape | solution.py:27
  39.2 2.5 fusion.3
  41.6 6.3 %reshape.34 = bf16[8,28,64,64]{3,2,0,1:T(8,128)(2,1)} reshape(bf16[8,28,4096]{2,0,1:T(8,128)(2,1)} %fusion.3) | data formatting | bytes 3670016 | tf_op jit(solution)/shard_map/reshape | solution.py:26
  47.9 6.2 %copy.32 = bf16[8,28,64,64]{2,0,3,1:T(8,128)(2,1)} copy(bf16[8,28,64,64]{3,2,0,1:T(8,128)(2,1)} %reshape.34) | data formatting | bytes 3670016 | tf_op jit(solution)/shard_map/reshape | solution.py:26
  54.1 5.9 %reshape.35 = bf16[512,1792]{0,1:T(8,128)(2,1)} reshape(bf16[8,64,28,64]{1,0,3,2:T(8,128)(2,1)} %bitcast.31) | data formatting | bytes 3670016 | tf_op jit(solution)/shard_map/reshape | solution.py:27
  60.0 0.6 all-to-all-done
  60.6 13.1 %fusion = bf16[2048,3584]{0,1:T(8,128)(2,1)} fusion(bf16[2048,512]{1,0:T(8,128)(2,1)S(1)} %bitcast.33, bf16[512,1792]{0,1:T(8,128)(2,1)} %reshape.35, bf16[512,1792]{0,1:T(8,128)(2,1)} %reshape.33), kind=kOutput, calls=%fused_computation.1 | convolution fusion | flops 7530872832 | bytes 20447232 | tf_op jit(solution)/shard_map/dot_general | solution.py:59
  73.7 18.8 %copy.37 = bf16[2048,3584]{1,0:T(8,128)(2,1)} copy(bf16[2048,3584]{0,1:T(8,128)(2,1)} %fusion) | data formatting | bytes 29360128
  92.6 198.2 %reduce-scatter.7.cloned.1.call-done = bf16[128,3584]{1,0:T(8,128)(2,1)} async-done(((bf16[2048,3584]{1,0:T(8,128)(2,1)}), bf16[128,3584]{1,0:T(8,128)(2,1)}) %reduce-scatter.7.cloned.1.call-update) | async-done | bytes 917520
  290.8 1.5 copy.38
  292.5 1.0 fusion.8
  294.1 1.3 fusion.1
  295.4 1.0 copy.35
  296.4 4.9 %reshape.37 = bf16[28,8,64,64]{3,2,1,0:T(8,128)(2,1)} reshape(bf16[28,8,4096]{2,1,0:T(8,128)(2,1)S(1)} %copy.35) | data formatting | bytes 3670016 | tf_op jit(solution)/shard_map/reshape | solution.py:26
  301.4 7.5 %copy.36 = bf16[28,64,8,64]{3,2,1,0:T(8,128)(2,1)} copy(bf16[28,64,8,64]{3,1,2,0:T(8,128)(2,1)} %bitcast.32) | data formatting | bytes 3670016 | tf_op jit(solution)/shard_map/transpose | solution.py:26
  308.9 5.0 %reshape.38 = bf16[1792,512]{1,0:T(8,128)(2,1)S(1)} reshape(bf16[28,64,8,64]{3,2,1,0:T(8,128)(2,1)} %copy.36) | data formatting | bytes 3670016 | tf_op jit(solution)/shard_map/reshape | solution.py:27
  313.9 79.6 %all-gather.2.cloned.1.call-done = bf16[2048,1792]{0,1:T(8,128)(2,1)} async-done(((bf16[128,1792]{0,1:T(8,128)(2,1)}), bf16[2048,1792]{0,1:T(8,128)(2,1)}) %all-gather.2.cloned.1.call-update) | async-done | bytes 7340048 | tf_op jit(solution)/shard_map/all_gather | solution.py:65
  393.5 8.6 %convolution_convert_fusion.4 = bf16[2048,512]{1,0:T(8,128)(2,1)} fusion(bf16[2048,1792]{0,1:T(8,128)(2,1)} %all-gather.2.cloned.1.call-done, bf16[1792,512]{1,0:T(8,128)(2,1)S(1)} %reshape.38), kind=kOutput, calls=%fused_computation.11 | convolution fusion | flops 3759144960 | bytes 11272192 | tf_op jit(solution)/shard_map/dot_general | solution.py:68
  402.1 84.5 %reduce-scatter.5.cloned.1.call-done = bf16[128,512]{1,0:T(8,128)(2,1)} async-done(((bf16[2048,512]{1,0:T(8,128)(2,1)}), bf16[128,512]{1,0:T(8,128)(2,1)}) %reduce-scatter.5.cloned.1.call-update) | async-done | bytes 131088 | tf_op jit(solution)/shard_map/reduce_scatter | solution.py:67
  (33 shorter events, 1.2 us)
Async XLA Ops:
  9.0 8.7 %copy-start.3 = (s32[28,4]{0,1:T(4,128)S(1)}, s32[28,4]{0,1:T(4,128)}, u32[]{:S(2)}) copy-start(s32[28,4]{0,1:T(4,128)} %param.16) | copy-start | bytes 1348
  9.0 8.7 %copy-start.4 = (s32[28,4]{0,1:T(4,128)S(1)}, s32[28,4]{0,1:T(4,128)}, u32[]{:S(2)}) copy-start(s32[28,4]{0,1:T(4,128)} %param.13) | copy-start | bytes 1348
  9.0 8.8 %copy-start.5 = (f32[28,4]{0,1:T(4,128)S(1)}, f32[28,4]{0,1:T(4,128)}, u32[]{:S(2)}) copy-start(f32[28,4]{0,1:T(4,128)} %param.12) | copy-start | bytes 1348
  9.0 8.9 %copy-start.7 = (bf16[28,4,4096]{2,1,0:T(4,128)(2,1)S(1)}, bf16[28,4,4096]{2,1,0:T(4,128)(2,1)}, u32[]{:S(2)}) copy-start(bf16[28,4,4096]{2,1,0:T(4,128)(2,1)} %param.11) | copy-start | bytes 2752516
  9.1 51.6 %all-to-all-start = ((bf16[16,128,512]{2,1,0:T(8,128)(2,1)}), bf16[16,128,512]{2,1,0:T(8,128)(2,1)S(1)}, u32[]{:S(2)}, u32[]{:S(2)}) async-start(bf16[16,128,512]{2,1,0:T(8,128)(2,1)} %stack.2), calls=%async_computation | async-start | bytes 4194304 | tf_op jit(solution)/shard_map/all_to_all | solution.py:8
  17.7 273.1 %reduce-scatter.7.cloned.1.call-start = ((), (), s32[]{:S(2)}) async-start(), calls=%async_computation.5 | async-start | bytes 15597568
  32.9 6.1 %copy-start.6 = (f32[28,4]{0,1:T(4,128)S(1)}, f32[28,4]{0,1:T(4,128)}, u32[]{:S(2)}) copy-start(f32[28,4]{0,1:T(4,128)} %param.15) | copy-start | bytes 1348
  32.9 6.2 %copy-start.8 = (bf16[28,4,4096]{2,1,0:T(4,128)(2,1)S(1)}, bf16[28,4,4096]{2,1,0:T(4,128)(2,1)}, u32[]{:S(2)}) copy-start(bf16[28,4,4096]{2,1,0:T(4,128)(2,1)} %param.14) | copy-start | bytes 2752516
  92.5 301.0 %all-gather.2.cloned.1.call-start = ((), (), s32[]{:S(2)}) async-start(), calls=%async_computation.3 | async-start | bytes 7798784 | tf_op jit(solution)/shard_map/all_gather | solution.py:65
  292.3 1.4 copy-start.1
  292.3 1.5 copy-start.2
  292.3 1.5 copy-start
  293.5 193.1 %reduce-scatter.5.cloned.1.call-start = ((), (), s32[]{:S(2)}) async-start(), calls=%async_computation.4 | async-start | bytes 2228224 | tf_op jit(solution)/shard_map/reduce_scatter | solution.py:67
Sparse Core Ops, SparseCore 0:
  92.7 198.0 reduce-scatter.6
  293.6 99.8 all-gather.1
  402.2 84.3 reduce-scatter.4
